TPU v7x, 32 devices: a whole 2x2x4 slice. The times are simulated.
32 devices in a mesh: grp: 2 (over y), seq: 16 (over z, x, core).
Axes of the slice: x: 2, y: 2, z: 4, core: 2. Of those that a mesh axis runs over, the one named last changes fastest.
Arguments:
- queries: bfloat16 [4096, 128], P(('grp', 'seq')), parts along dimension 0, may hold values from -6 to 6
- keys: bfloat16 [4096, 128], P(('grp', 'seq')), parts along dimension 0, may hold values from -6 to 6
- values: bfloat16 [4096, 128], P(('grp', 'seq')), parts along dimension 0, may hold values from -6 to 6
- log_gate: float32 [4096], P(('grp', 'seq')), parts along dimension 0, may hold values from -1 to 0, as said below
- out_grad: bfloat16 [4096, 128], P(('grp', 'seq')), parts along dimension 0, may hold values from -6 to 6
- segment_order: int32 [64], P(('grp', 'seq')), parts along dimension 0, may hold values from 0 to 31, each once
Outputs:
- attn_out: bfloat16 [4096, 128], P(('grp', 'seq')), parts along dimension 0
- query_grad: float32 [4096, 128], P(('grp', 'seq')), parts along dimension 0
- key_grad: float32 [4096, 128], P(('grp', 'seq')), parts along dimension 0
- value_grad: float32 [4096, 128], P(('grp', 'seq')), parts along dimension 0
- gate_grad: float32 [4096], P(('grp', 'seq')), parts along dimension 0
There are 2 independent parts, one for each index of `grp`. A program takes and returns all parts, laid end to end along the dimension named above; each array names one. Nothing has to cross between parts.
Inputs may be any that keep to these rules, and one draw needn't show every extreme that they name: `log_gate`: every gate is below one. `segment_order`: each segment index appears once.
All inputs are finite; a program needn't handle non-finite values.
Results may differ from a plain program's by a relative error of at most 0.0095.
Values may be sent and summed in bfloat16 or wider, within the bound.
No kernel may reach another device: no remote copies, remote signals or barrier semaphores. Data moves between devices by JAX's collectives and lax.ppermute only.
A program may use at most 64 MiB of HBM per device.

v0:
```python
import jax
import jax.numpy as jnp
from jax import lax
from jax.sharding import PartitionSpec as P

masked_value = -1e30


def contract_last(left, right):
    return lax.dot_general(
        left, right, (((1,), (1,)), ((), ())), preferred_element_type=jnp.float32
    )


def contract_first(left, right):
    return lax.dot_general(
        left, right, (((0,), (0,)), ((), ())), preferred_element_type=jnp.float32
    )


def tile_scores(query_rows, query_gate, query_pos, key_rows, key_gate, key_pos, score_scale):
    scores = (
        contract_last(query_rows, key_rows) * score_scale + query_gate[:, None] - key_gate[None, :]
    )
    visible = key_pos[None, :] <= query_pos[:, None]
    return (scores, visible)


def tile_probs(scores, visible, row_total):
    return jnp.where(visible, jnp.exp(scores - row_total[:, None]), 0.0)


def local(queries, keys, values, log_gate, out_grad, segment_order):
    tokens_here, width = queries.shape
    devices = lax.axis_size("seq")
    segment_rows = tokens_here // 2
    total_len = tokens_here * devices
    score_scale = width ** (-0.5)
    offsets_in = lax.broadcasted_iota(jnp.int32, (1, segment_rows), 1)
    local_cum = jnp.cumsum(log_gate.reshape(2, segment_rows), axis=1)
    segment_total = local_cum[:, -1]
    segment_place = segment_order.astype(jnp.float32)
    own_pos = (segment_order[:, None] * segment_rows + offsets_in).reshape(-1)
    all_totals, all_place = (
        lax.all_gather(segment_total, "seq", axis=0, tiled=True),
        lax.all_gather(segment_place, "seq", axis=0, tiled=True),
    )
    earlier = (all_place[None, :] < segment_place[:, None]).astype(jnp.float32)
    own_offset = jnp.sum(earlier * all_totals[None, :], axis=1)
    own_gate = (local_cum + own_offset[:, None]).reshape(-1)
    all_gate = lax.all_gather(own_gate, "seq", axis=0, tiled=True)
    all_pos = (all_place.astype(jnp.int32)[:, None] * segment_rows + offsets_in).reshape(-1)
    key_all, value_all = (
        lax.all_gather(keys, "seq", axis=0, tiled=True),
        lax.all_gather(values, "seq", axis=0, tiled=True),
    )
    block = 2048
    count = total_len // block

    def key_tile(block_index):
        start = block_index * block
        return (
            lax.dynamic_slice_in_dim(key_all, start, block),
            lax.dynamic_slice_in_dim(value_all, start, block),
            lax.dynamic_slice_in_dim(all_gate, start, block),
            lax.dynamic_slice_in_dim(all_pos, start, block),
        )

    def stats_step(block_index, carry):
        run_max, run_sum = carry
        key_rows, value_rows, key_gate, key_pos = key_tile(block_index)
        scores, visible = tile_scores(
            queries, own_gate, own_pos, key_rows, key_gate, key_pos, score_scale
        )
        kept = jnp.where(visible, scores, masked_value)
        new_max = jnp.maximum(run_max, jnp.max(kept, axis=1))
        fresh = jnp.sum(jnp.where(visible, jnp.exp(kept - new_max[:, None]), 0.0), axis=1)
        return (new_max, run_sum * jnp.exp(run_max - new_max) + fresh)

    start_max = jnp.full((tokens_here,), masked_value, jnp.float32)
    run_max, run_sum = lax.fori_loop(
        0, count, stats_step, (start_max, jnp.zeros((tokens_here,), jnp.float32))
    )
    log_total = run_max + jnp.log(run_sum)

    def output_step(block_index, total):
        key_rows, value_rows, key_gate, key_pos = key_tile(block_index)
        scores, visible = tile_scores(
            queries, own_gate, own_pos, key_rows, key_gate, key_pos, score_scale
        )
        probs = tile_probs(scores, visible, log_total).astype(jnp.bfloat16)
        return total + jnp.dot(probs, value_rows, preferred_element_type=jnp.float32)

    out_full = lax.fori_loop(0, count, output_step, jnp.zeros((tokens_here, width), jnp.float32))
    attn_out = out_full.astype(jnp.bfloat16)
    row_delta = jnp.sum(out_grad.astype(jnp.float32) * out_full, axis=1)

    def row_terms(block_index):
        key_rows, value_rows, key_gate, key_pos = key_tile(block_index)
        scores, visible = tile_scores(
            queries, own_gate, own_pos, key_rows, key_gate, key_pos, score_scale
        )
        probs = tile_probs(scores, visible, log_total)
        dprob = contract_last(out_grad, value_rows)
        return (key_rows, probs, probs * (dprob - row_delta[:, None]))

    def query_step(block_index, total):
        key_rows, probs, dscore = row_terms(block_index)
        return total + jnp.dot(
            dscore.astype(jnp.bfloat16), key_rows, preferred_element_type=jnp.float32
        )

    query_acc = lax.fori_loop(0, count, query_step, jnp.zeros((tokens_here, width), jnp.float32))
    query_all, grad_all = (
        lax.all_gather(queries, "seq", axis=0, tiled=True),
        lax.all_gather(out_grad, "seq", axis=0, tiled=True),
    )
    total_all, delta_all = (
        lax.all_gather(log_total, "seq", axis=0, tiled=True),
        lax.all_gather(row_delta, "seq", axis=0, tiled=True),
    )

    def column_step(block_index, carry):
        key_acc, value_acc, column_acc = carry
        start = block_index * block
        query_rows = lax.dynamic_slice_in_dim(query_all, start, block)
        grad_rows = lax.dynamic_slice_in_dim(grad_all, start, block)
        scores, visible = tile_scores(
            query_rows,
            lax.dynamic_slice_in_dim(all_gate, start, block),
            lax.dynamic_slice_in_dim(all_pos, start, block),
            keys,
            own_gate,
            own_pos,
            score_scale,
        )
        probs = tile_probs(scores, visible, lax.dynamic_slice_in_dim(total_all, start, block))
        dprob = contract_last(grad_rows, values)
        dscore = probs * (dprob - lax.dynamic_slice_in_dim(delta_all, start, block)[:, None])
        dscore_low = dscore.astype(jnp.bfloat16)
        key_acc = key_acc + contract_first(dscore_low, query_rows) * score_scale
        value_acc = value_acc + contract_first(probs.astype(jnp.bfloat16), grad_rows)
        column_acc = column_acc - jnp.sum(dscore, axis=0)
        return (key_acc, value_acc, column_acc)

    zeros_own = jnp.zeros((tokens_here, width), jnp.float32)
    key_grad, value_grad, gate_point = lax.fori_loop(
        0, count, column_step, (zeros_own, zeros_own, jnp.zeros((tokens_here,), jnp.float32))
    )
    query_grad = query_acc * score_scale
    point_rows = gate_point.reshape(2, segment_rows)
    within = jnp.flip(jnp.cumsum(jnp.flip(point_rows, 1), axis=1), 1)
    all_point = lax.all_gather(within[:, 0], "seq", axis=0, tiled=True)
    later = (all_place[None, :] > segment_place[:, None]).astype(jnp.float32)
    gate_grad = (within + jnp.sum(later * all_point[None, :], axis=1)[:, None]).reshape(-1)
    return (attn_out, query_grad, key_grad, value_grad, gate_grad)


def solution(mesh):
    placed = (
        P(("grp", "seq"), None),
        P(("grp", "seq"), None),
        P(("grp", "seq"), None),
        P(("grp", "seq")),
        P(("grp", "seq"), None),
        P(("grp", "seq")),
    )
    return jax.shard_map(
        local,
        mesh=mesh,
        in_specs=placed,
        out_specs=(
            P(("grp", "seq"), None),
            P(("grp", "seq"), None),
            P(("grp", "seq"), None),
            P(("grp", "seq"), None),
            P(("grp", "seq")),
        ),
        check_vma=False,
    )
```

profile of v0, /device:TPU:0, one launch (start us, length us, event | category | flops | bytes accessed | tf_op | source)
XLA Modules:
  0.0 211.5 jit_solution(15644140626693972713)
XLA Ops:
  0.6 0.0 copy-start
  0.6 0.9 copy.17
  1.5 0.0 copy-done
  1.5 0.0 copy-start.4
  1.5 24.6 %all_gather.34 = bf16[2048,128]{1,0:T(8,128)(2,1)S(1)} all-gather(bf16[128,128]{1,0:T(8,128)(2,1)S(1)} %copy-done), channel_id=1, replica_groups=mesh['grp'=2,'seq'=16] {'seq'}, dimensions={0}, use_global_device_ids=true | all-gather | bytes 557056 | tf_op jit(solution)/shard_map/all_gather | solution.py:55
  26.1 0.0 copy-done.4
  26.2 0.1 reshape.129
  26.2 0.2 reduce_window_sum.17
  26.5 0.2 slice_reduce_fusion.1
  26.7 0.0 copy-start.6
  26.7 0.6 copy-done.6
  27.3 0.6 dynamic-slice
  28.6 0.2 dynamic-update-slice.1
  28.8 0.0 copy-start.5
  28.8 0.7 copy-done.5
  29.5 0.1 convert_dynamic-update-slice_fusion
  29.5 29.8 %all-reduce.3 = (f32[32]{0:T(128)S(1)}, f32[32]{0:T(128)S(1)}) all-reduce(f32[32]{0:T(128)S(1)} %dynamic-update-slice.1, f32[32]{0:T(128)S(1)} %convert_dynamic-update-slice_fusion), channel_id=2, replica_groups=mesh['grp'=2,'seq'=16] {'seq'}, use_global_device_ids=true, to_apply=%add.1 | all-reduce | flops 64 | bytes 512
  59.4 0.0 copy-start.3
  59.4 0.1 iota_add_fusion
  59.4 0.1 add.179
  59.5 0.1 iota_add_fusion.1
  59.6 0.1 add.183
  59.7 0.2 fusion.29
  59.9 0.1 broadcast_add_fusion.1
  59.9 0.1 reshape.142
  60.0 17.1 %all-gather.2 = f32[16,1,128]{2,1,0:T(1,128)S(1)} all-gather(f32[1,1,128]{2,1,0:T(1,128)S(1)} %reshape.142), channel_id=1, replica_groups=mesh['grp'=2,'seq'=16] {'seq'}, dimensions={0}, use_global_device_ids=true | all-gather | bytes 8704 | tf_op jit(solution)/shard_map/all_gather | solution.py:51
  77.2 0.1 add.186
  77.2 0.0 copy-done.3
  77.2 0.0 copy-start.2
  77.2 20.7 %all_gather.31 = bf16[2048,128]{1,0:T(8,128)(2,1)S(1)} all-gather(bf16[128,128]{1,0:T(8,128)(2,1)S(1)} %copy-done.3), channel_id=1, replica_groups=mesh['grp'=2,'seq'=16] {'seq'}, dimensions={0}, use_global_device_ids=true | all-gather | bytes 557056 | tf_op jit(solution)/shard_map/all_gather | solution.py:54
  98.0 0.0 copy-done.2
  98.0 0.5 fusion.13
  98.4 0.4 fusion.12
  98.8 0.5 multiply_reduce_fusion
  99.3 0.0 copy-start.1
  99.3 0.7 copy.18
  100.0 0.0 copy-done.1
  100.1 1.2 fusion.11
  101.3 18.9 %all_gather.35 = bf16[2048,128]{1,0:T(8,128)(2,1)S(1)} all-gather(bf16[128,128]{1,0:T(8,128)(2,1)S(1)} %copy-done.2), channel_id=1, replica_groups=mesh['grp'=2,'seq'=16] {'seq'}, dimensions={0}, use_global_device_ids=true | all-gather | bytes 557056 | tf_op jit(solution)/shard_map/all_gather | solution.py:115
  120.1 18.8 %all-gather.3 = f32[16,1,128]{2,1,0:T(1,128)S(1)} all-gather(f32[1,1,128]{2,1,0:T(1,128)S(1)} %bitcast.24), channel_id=1, replica_groups=mesh['grp'=2,'seq'=16] {'seq'}, dimensions={0}, use_global_device_ids=true | all-gather | bytes 8704 | tf_op jit(solution)/shard_map/all_gather | solution.py:119
  138.9 0.9 fusion.5
  139.8 17.4 %all-gather.4 = f32[16,1,128]{2,1,0:T(1,128)S(1)} all-gather(f32[1,1,128]{2,1,0:T(1,128)S(1)} %bitcast.23), channel_id=1, replica_groups=mesh['grp'=2,'seq'=16] {'seq'}, dimensions={0}, use_global_device_ids=true | all-gather | bytes 8704 | tf_op jit(solution)/shard_map/all_gather | solution.py:120
  157.2 20.3 %all_gather.37 = bf16[2048,128]{1,0:T(8,128)(2,1)S(1)} all-gather(bf16[128,128]{1,0:T(8,128)(2,1)S(1)} %copy-done.1), channel_id=1, replica_groups=mesh['grp'=2,'seq'=16] {'seq'}, dimensions={0}, use_global_device_ids=true | all-gather | bytes 557056 | tf_op jit(solution)/shard_map/all_gather | solution.py:116
  177.5 0.4 fusion.33
  178.0 1.0 convolution_multiply_fusion.2
  178.9 1.0 fusion.17
  179.9 0.1 reduce_sum.53
  180.0 0.1 reverse.4
  180.1 0.2 reduce_window_sum.18
  180.3 0.1 rev.8
  180.4 0.2 slice_reduce_fusion
  180.6 0.2 dynamic-update-slice.2
  180.9 29.8 %all-reduce.2 = f32[32]{0:T(128)S(1)} all-reduce(f32[32]{0:T(128)S(1)} %dynamic-update-slice.2), channel_id=3, replica_groups=mesh['grp'=2,'seq'=16] {'seq'}, use_global_device_ids=true, to_apply=%add.2 | all-reduce | flops 32 | bytes 256
  210.7 0.2 fusion.30
  210.9 0.1 broadcast_add_fusion
  210.9 0.6 reshape.130
  (8 shorter events, 0.0 us)
Async XLA Ops:
  0.6 0.9 copy-start
  1.5 24.6 %copy-start.4 = (f32[128]{0:T(128)S(1)}, f32[128]{0:T(128)}, u32[]{:S(2)}) copy-start(f32[128]{0:T(128)} %param.9) | copy-start | bytes 1540
  26.7 0.7 copy-start.6
  28.8 0.7 copy-start.5
  59.4 17.9 %copy-start.3 = (bf16[128,128]{1,0:T(8,128)(2,1)S(1)}, bf16[128,128]{1,0:T(8,128)(2,1)}, u32[]{:S(2)}) copy-start(bf16[128,128]{1,0:T(8,128)(2,1)} %param.7) | copy-start | bytes 98308
  77.2 20.7 %copy-start.2 = (bf16[128,128]{1,0:T(8,128)(2,1)S(1)}, bf16[128,128]{1,0:T(8,128)(2,1)}, u32[]{:S(2)}) copy-start(bf16[128,128]{1,0:T(8,128)(2,1)} %param.6) | copy-start | bytes 98308
  99.3 0.8 copy-start.1
where the time goes:
time: 212 us
  blocking collectives  197 us (93%)
  local copies, waits for them, and re-layouts  5.65 us (3%)
  matrix products  5.38 us (3%)
    unnamed x2, blocking collectives  59.6 us
    all_gather x1, blocking collectives, local(): lax.all_gather(values, 'seq', axis=0, tiled=True)  24.6 us
    all_gather x1, blocking collectives, local(): lax.all_gather(keys, 'seq', axis=0, tiled=True)  20.7 us
    all_gather x1, blocking collectives, local(): lax.all_gather(out_grad, 'seq', axis=0, tiled=True)  20.3 us
    all_gather x1, blocking collectives, local(): lax.all_gather(queries, 'seq', axis=0, tiled=True)  18.9 us
    all_gather x1, blocking collectives, local(): lax.all_gather(log_total, 'seq', axis=0, tiled=True)  18.8 us
    all_gather x1, blocking collectives, local(): lax.all_gather(row_delta, 'seq', axis=0, tiled=True)  17.4 us
    all_gather x1, blocking collectives, local(): all_gate = lax.all_gather(own_gate, 'seq', axis=0, tiled=True)  17.1 us

commit v1 on v0

--- a/solution.py
+++ b/solution.py
@@ -48,7 +48,12 @@
     earlier = (all_place[None, :] < segment_place[:, None]).astype(jnp.float32)
     own_offset = jnp.sum(earlier * all_totals[None, :], axis=1)
     own_gate = (local_cum + own_offset[:, None]).reshape(-1)
-    all_gate = lax.all_gather(own_gate, "seq", axis=0, tiled=True)
+    ring = [own_gate]
+    for hop in range(15):
+        ring.append(lax.ppermute(ring[-1], "seq", [(dev, (dev + 1) % 16) for dev in range(16)]))
+    all_gate = jnp.roll(
+        jnp.concatenate(ring[::-1], axis=0), (lax.axis_index("seq") + 1) * ring[0].shape[0], axis=0
+    )
     all_pos = (all_place.astype(jnp.int32)[:, None] * segment_rows + offsets_in).reshape(-1)
     key_all, value_all = (
         lax.all_gather(keys, "seq", axis=0, tiled=True),

time: 212 us -> 264 us (1.25)
  waiting for transfers between devices: 0 us -> 61.5 us
  blocking collectives: 197 us -> 182 us
  matrix products: 5.38 us -> 9.15 us
    ppermute x0 -> x15, waiting for transfers between devices: none -> 61.5 us  [local(): lax.ppermute(ring[-1], 'seq', [(dev, (dev + 1) % 16) for dev in range(16)])]
    all_gather x1 -> x0, blocking collectives: 17.1 us -> none  [local(): all_gate = lax.all_gather(own_gate, 'seq', axis=0, tiled=True)]
    unnamed x2, blocking collectives: 59.6 us -> 64.7 us
    all_gather x1, blocking collectives: 24.6 us -> 21.8 us  [local(): lax.all_gather(values, 'seq', axis=0, tiled=True)]
  transfers between devices with their start and end apart: 0 -> 15, of which waited for: 0 -> 11; matrix products, arithmetic and copies ran while one was open for 0% -> 0% of each run, Pallas kernels for 0% -> 0%
where the time goes in v1:
time: 264 us; the launch traced here: 263 us
  blocking collectives  182 us (69%)
  waiting for transfers between devices  61.5 us (23%)
  matrix products  9.15 us (3%)
  local copies, waits for them, and re-layouts  4.94 us (2%)
  other arithmetic  3.09 us (1%)
    unnamed x2, blocking collectives  64.7 us
    ppermute x15, waiting for transfers between devices, local(): lax.ppermute(ring[-1], 'seq', [(dev, (dev + 1) % 16) for dev in range(16)])  61.5 us
    all_gather x1, blocking collectives, local(): lax.all_gather(values, 'seq', axis=0, tiled=True)  21.8 us
    all_gather x1, blocking collectives, local(): lax.all_gather(out_grad, 'seq', axis=0, tiled=True)  20.5 us
    all_gather x1, blocking collectives, local(): lax.all_gather(queries, 'seq', axis=0, tiled=True)  19.4 us
    all_gather x1, blocking collectives, local(): lax.all_gather(keys, 'seq', axis=0, tiled=True)  19.4 us
    all_gather x1, blocking collectives, local(): lax.all_gather(log_total, 'seq', axis=0, tiled=True)  19.1 us
    all_gather x1, blocking collectives, local(): lax.all_gather(row_delta, 'seq', axis=0, tiled=True)  17.1 us
  transfers between devices with their start and end apart: 15, of which 11 were waited for; matrix products, arithmetic and copies ran while one was open for 0% of the time, Pallas kernels for 0%

profile of v1, /device:TPU:0, one launch (start us, length us, event | category | flops | bytes accessed | tf_op | source)
XLA Modules:
  0.0 263.2 jit_solution(4911089004829261858)
XLA Ops:
  0.6 0.0 copy-start.6
  0.7 0.7 reshape.129
  1.4 0.2 reduce_window_sum.17
  1.6 0.2 slice_reduce_fusion.1
  1.8 0.7 broadcast_multiply_fusion
  2.6 0.6 dynamic-slice
  3.8 0.8 convert_dynamic-update-slice_fusion
  4.6 0.2 dynamic-update-slice.1
  4.8 34.9 %all-reduce.3 = (f32[32]{0:T(128)S(1)}, f32[32]{0:T(128)S(1)}) all-reduce(f32[32]{0:T(128)S(1)} %dynamic-update-slice.1, f32[32]{0:T(128)S(1)} %convert_dynamic-update-slice_fusion), channel_id=2, replica_groups=mesh['grp'=2,'seq'=16] {'seq'}, use_global_device_ids=true, to_apply=%add.1 | all-reduce | flops 64 | bytes 512
  39.7 0.2 fusion.21
  39.9 0.1 broadcast_add_fusion.1
  39.9 0.1 add.199
  40.0 5.7 %collective-permute-done = f32[128]{0:T(128)S(1)} collective-permute-done((f32[128]{0:T(128)S(1)}, f32[128]{0:T(128)S(1)}, u32[]{:S(2)}, u32[]{:S(2)}) %collective-permute-start) | collective-permute-done | bytes 544 | tf_op jit(solution)/shard_map/ppermute | solution.py:53
  45.7 5.7 %collective-permute-done.1 = f32[128]{0:T(128)S(1)} collective-permute-done((f32[128]{0:T(128)S(1)}, f32[128]{0:T(128)S(1)}, u32[]{:S(2)}, u32[]{:S(2)}) %collective-permute-start.1) | collective-permute-done | bytes 544 | tf_op jit(solution)/shard_map/ppermute | solution.py:53
  51.4 5.7 %collective-permute-done.2 = f32[128]{0:T(128)S(1)} collective-permute-done((f32[128]{0:T(128)S(1)}, f32[128]{0:T(128)S(1)}, u32[]{:S(2)}, u32[]{:S(2)}) %collective-permute-start.2) | collective-permute-done | bytes 544 | tf_op jit(solution)/shard_map/ppermute | solution.py:53
  57.1 5.7 %collective-permute-done.3 = f32[128]{0:T(128)S(1)} collective-permute-done((f32[128]{0:T(128)S(1)}, f32[128]{0:T(128)S(1)}, u32[]{:S(2)}, u32[]{:S(2)}) %collective-permute-start.3) | collective-permute-done | bytes 544 | tf_op jit(solution)/shard_map/ppermute | solution.py:53
  62.8 19.4 %all_gather.31 = bf16[2048,128]{1,0:T(8,128)(2,1)S(1)} all-gather(bf16[128,128]{1,0:T(8,128)(2,1)S(1)} %copy-done.4), channel_id=1, replica_groups=mesh['grp'=2,'seq'=16] {'seq'}, dimensions={0}, use_global_device_ids=true | all-gather | bytes 557056 | tf_op jit(solution)/shard_map/all_gather | solution.py:120
  82.2 0.2 collective-permute-start.5
  82.4 0.3 convolution_multiply_fusion
  82.7 0.0 copy-start.5
  82.7 5.2 %collective-permute-done.5 = f32[128]{0:T(128)S(1)} collective-permute-done((f32[128]{0:T(128)S(1)}, f32[128]{0:T(128)S(1)}, u32[]{:S(2)}, u32[]{:S(2)}) %collective-permute-start.5) | collective-permute-done | bytes 544 | tf_op jit(solution)/shard_map/ppermute | solution.py:53
  87.9 0.0 collective-permute-start.6
  87.9 19.4 %all_gather.28 = bf16[2048,128]{1,0:T(8,128)(2,1)S(1)} all-gather(bf16[128,128]{1,0:T(8,128)(2,1)S(1)} %copy-done.2), channel_id=1, replica_groups=mesh['grp'=2,'seq'=16] {'seq'}, dimensions={0}, use_global_device_ids=true | all-gather | bytes 557056 | tf_op jit(solution)/shard_map/all_gather | solution.py:59
  107.3 0.2 collective-permute-start.7
  107.5 21.8 %all_gather.30 = bf16[2048,128]{1,0:T(8,128)(2,1)} all-gather(bf16[128,128]{1,0:T(8,128)(2,1)S(1)} %copy-done.5), channel_id=1, replica_groups=mesh['grp'=2,'seq'=16] {'seq'}, dimensions={0}, use_global_device_ids=true | all-gather | bytes 557056 | tf_op jit(solution)/shard_map/all_gather | solution.py:60
  129.3 0.3 collective-permute-start.8
  129.6 20.5 %all_gather.33 = bf16[2048,128]{1,0:T(8,128)(2,1)} all-gather(bf16[128,128]{1,0:T(8,128)(2,1)S(1)} %copy-done.3), channel_id=1, replica_groups=mesh['grp'=2,'seq'=16] {'seq'}, dimensions={0}, use_global_device_ids=true | all-gather | bytes 557056 | tf_op jit(solution)/shard_map/all_gather | solution.py:121
  150.1 0.2 collective-permute-start.9
  150.3 5.5 %collective-permute-done.9 = f32[128]{0:T(128)S(1)} collective-permute-done((f32[128]{0:T(128)S(1)}, f32[128]{0:T(128)S(1)}, u32[]{:S(2)}, u32[]{:S(2)}) %collective-permute-start.9) | collective-permute-done | bytes 544 | tf_op jit(solution)/shard_map/ppermute | solution.py:53
  155.8 0.1 iota_add_fusion
  155.9 5.6 %collective-permute-done.10 = f32[128]{0:T(128)S(1)} collective-permute-done((f32[128]{0:T(128)S(1)}, f32[128]{0:T(128)S(1)}, u32[]{:S(2)}, u32[]{:S(2)}) %collective-permute-start.10) | collective-permute-done | bytes 544 | tf_op jit(solution)/shard_map/ppermute | solution.py:53
  161.5 0.0 collective-permute-start.11
  161.5 0.1 iota_add_fusion.1
  161.6 5.6 %collective-permute-done.11 = f32[128]{0:T(128)S(1)} collective-permute-done((f32[128]{0:T(128)S(1)}, f32[128]{0:T(128)S(1)}, u32[]{:S(2)}, u32[]{:S(2)}) %collective-permute-start.11) | collective-permute-done | bytes 544 | tf_op jit(solution)/shard_map/ppermute | solution.py:53
  167.2 0.0 collective-permute-start.12
  167.2 0.1 copy.17
  167.3 5.6 %collective-permute-done.12 = f32[128]{0:T(128)S(1)} collective-permute-done((f32[128]{0:T(128)S(1)}, f32[128]{0:T(128)S(1)}, u32[]{:S(2)}, u32[]{:S(2)}) %collective-permute-start.12) | collective-permute-done | bytes 544 | tf_op jit(solution)/shard_map/ppermute | solution.py:53
  172.9 0.0 collective-permute-start.13
  172.9 5.7 %collective-permute-done.13 = f32[128]{0:T(128)S(1)} collective-permute-done((f32[128]{0:T(128)S(1)}, f32[128]{0:T(128)S(1)}, u32[]{:S(2)}, u32[]{:S(2)}) %collective-permute-start.13) | collective-permute-done | bytes 544 | tf_op jit(solution)/shard_map/ppermute | solution.py:53
  178.6 0.1 add.192
  178.6 0.1 add.196
  178.7 5.5 %collective-permute-done.14 = f32[128]{0:T(128)S(1)} collective-permute-done((f32[128]{0:T(128)S(1)}, f32[128]{0:T(128)S(1)}, u32[]{:S(2)}, u32[]{:S(2)}) %collective-permute-start.14) | collective-permute-done | bytes 544 | tf_op jit(solution)/shard_map/ppermute | solution.py:53
  184.7 0.1 dynamic_slice.38
  184.8 0.5 fusion.7
  185.2 0.4 fusion.6
  185.7 0.6 copy-done.1
  186.3 0.5 multiply_reduce_fusion
  186.8 2.3 fusion.5
  189.0 17.1 %all-gather.3 = f32[16,1,128]{2,1,0:T(1,128)S(1)} all-gather(f32[1,1,128]{2,1,0:T(1,128)S(1)} %bitcast.22), channel_id=1, replica_groups=mesh['grp'=2,'seq'=16] {'seq'}, dimensions={0}, use_global_device_ids=true | all-gather | bytes 8704 | tf_op jit(solution)/shard_map/all_gather | solution.py:125
  206.1 19.1 %all-gather.2 = f32[16,1,128]{2,1,0:T(1,128)S(1)} all-gather(f32[1,1,128]{2,1,0:T(1,128)S(1)} %bitcast.21), channel_id=1, replica_groups=mesh['grp'=2,'seq'=16] {'seq'}, dimensions={0}, use_global_device_ids=true | all-gather | bytes 8704 | tf_op jit(solution)/shard_map/all_gather | solution.py:124
  225.2 2.9 %fusion.19 = f32[128,128]{1,0:T(8,128)} fusion(bf16[2048,128]{1,0:T(8,128)(2,1)} %all_gather.33, f32[2048,128]{1,0:T(8,128)S(1)} %convolution_multiply_fusion, f32[2048]{0:T(1024)S(1)} %bitcast.19, f32[128]{0:T(128)S(1)} %add.199, f32[2048]{0:T(1024)S(1)} %dynamic_slice.38, s32[128]{0:T(128)S(1)} %add.196, s32[2048]{0:T(1024)S(1)} %add.192), kind=kOutput, calls=%fused_computation.27 | convolution fusion | flops 68681728 | bytes 1664000 | tf_op jit(solution)/shard_map/while/body/eval_jaxpr/dot_general | solution.py:16
  228.2 1.8 fusion.26
  229.9 0.1 reduce_sum.53
  230.0 0.1 reverse.4
  230.1 0.2 reduce_window_sum.18
  230.3 0.1 rev.8
  230.4 0.2 slice_reduce_fusion
  230.6 0.7 copy.18
  231.4 1.0 convolution_multiply_fusion.2
  232.3 0.2 dynamic-update-slice.2
  232.5 29.8 %all-reduce.2 = f32[32]{0:T(128)S(1)} all-reduce(f32[32]{0:T(128)S(1)} %dynamic-update-slice.2), channel_id=3, replica_groups=mesh['grp'=2,'seq'=16] {'seq'}, use_global_device_ids=true, to_apply=%add.2 | all-reduce | flops 32 | bytes 256
  262.3 0.2 fusion.22
  262.5 0.1 broadcast_add_fusion
  262.6 0.6 reshape.130
  (62 shorter events, 0.3 us)
Async XLA Ops:
  0.6 1.9 copy-start.6
  0.6 62.2 %copy-start.4 = (bf16[128,128]{1,0:T(8,128)(2,1)S(1)}, bf16[128,128]{1,0:T(8,128)(2,1)}, u32[]{:S(2)}) copy-start(bf16[128,128]{1,0:T(8,128)(2,1)} %param.6) | copy-start | bytes 98308
  40.0 42.4 %copy-start.2 = (bf16[128,128]{1,0:T(8,128)(2,1)S(1)}, bf16[128,128]{1,0:T(8,128)(2,1)}, u32[]{:S(2)}) copy-start(bf16[128,128]{1,0:T(8,128)(2,1)} %param.7) | copy-start | bytes 98308
  40.0 5.7 %collective-permute-start = (f32[128]{0:T(128)S(1)}, f32[128]{0:T(128)S(1)}, u32[]{:S(2)}, u32[]{:S(2)}) collective-permute-start(f32[128]{0:T(128)S(1)} %add.199), channel_id=1, source_target_pairs={{0,1},{1,2},{2,3},{3,4},{4,5},{5,6},{6,7},{7,8},{8,9},{9,10},{10,1... | collective-permute-start | bytes 1544 | tf_op jit(solution)/shard_map/ppermute | solution.py:53
  45.7 5.7 %collective-permute-start.1 = (f32[128]{0:T(128)S(1)}, f32[128]{0:T(128)S(1)}, u32[]{:S(2)}, u32[]{:S(2)}) collective-permute-start(f32[128]{0:T(128)S(1)} %collective-permute-done), channel_id=1, source_target_pairs={{0,1},{1,2},{2,3},{3,4},{4,5},{5,6},{6,7},{7,8},{8,9},{9,10},{10,1... | collective-permute-start | bytes 1544 | tf_op jit(solution)/shard_map/ppermute | solution.py:53
  51.4 5.7 %collective-permute-start.2 = (f32[128]{0:T(128)S(1)}, f32[128]{0:T(128)S(1)}, u32[]{:S(2)}, u32[]{:S(2)}) collective-permute-start(f32[128]{0:T(128)S(1)} %collective-permute-done.1), channel_id=1, source_target_pairs={{0,1},{1,2},{2,3},{3,4},{4,5},{5,6},{6,7},{7,8},{8,9},{9,10},{10,1... | collective-permute-start | bytes 1544 | tf_op jit(solution)/shard_map/ppermute | solution.py:53
  57.1 5.7 %collective-permute-start.3 = (f32[128]{0:T(128)S(1)}, f32[128]{0:T(128)S(1)}, u32[]{:S(2)}, u32[]{:S(2)}) collective-permute-start(f32[128]{0:T(128)S(1)} %collective-permute-done.2), channel_id=1, source_target_pairs={{0,1},{1,2},{2,3},{3,4},{4,5},{5,6},{6,7},{7,8},{8,9},{9,10},{10,1... | collective-permute-start | bytes 1544 | tf_op jit(solution)/shard_map/ppermute | solution.py:53
  62.8 19.4 %collective-permute-start.4 = (f32[128]{0:T(128)S(1)}, f32[128]{0:T(128)S(1)}, u32[]{:S(2)}, u32[]{:S(2)}) collective-permute-start(f32[128]{0:T(128)S(1)} %collective-permute-done.3), channel_id=1, source_target_pairs={{0,1},{1,2},{2,3},{3,4},{4,5},{5,6},{6,7},{7,8},{8,9},{9,10},{10,1... | collective-permute-start | bytes 1544 | tf_op jit(solution)/shard_map/ppermute | solution.py:53
  82.2 5.7 %collective-permute-start.5 = (f32[128]{0:T(128)S(1)}, f32[128]{0:T(128)S(1)}, u32[]{:S(2)}, u32[]{:S(2)}) collective-permute-start(f32[128]{0:T(128)S(1)} %collective-permute-done.4), channel_id=1, source_target_pairs={{0,1},{1,2},{2,3},{3,4},{4,5},{5,6},{6,7},{7,8},{8,9},{9,10},{10,1... | collective-permute-start | bytes 1544 | tf_op jit(solution)/shard_map/ppermute | solution.py:53
  82.7 24.8 %copy-start.5 = (bf16[128,128]{1,0:T(8,128)(2,1)S(1)}, bf16[128,128]{1,0:T(8,128)(2,1)}, u32[]{:S(2)}) copy-start(bf16[128,128]{1,0:T(8,128)(2,1)} %param.8) | copy-start | bytes 98308
  87.9 19.4 %collective-permute-start.6 = (f32[128]{0:T(128)S(1)}, f32[128]{0:T(128)S(1)}, u32[]{:S(2)}, u32[]{:S(2)}) collective-permute-start(f32[128]{0:T(128)S(1)} %collective-permute-done.5), channel_id=1, source_target_pairs={{0,1},{1,2},{2,3},{3,4},{4,5},{5,6},{6,7},{7,8},{8,9},{9,10},{10,1... | collective-permute-start | bytes 1544 | tf_op jit(solution)/shard_map/ppermute | solution.py:53
  107.3 22.3 %copy-start.3 = (bf16[128,128]{1,0:T(8,128)(2,1)S(1)}, bf16[128,128]{1,0:T(8,128)(2,1)}, u32[]{:S(2)}) copy-start(bf16[128,128]{1,0:T(8,128)(2,1)} %param.10) | copy-start | bytes 98308
  107.3 21.9 %collective-permute-start.7 = (f32[128]{0:T(128)S(1)}, f32[128]{0:T(128)S(1)}, u32[]{:S(2)}, u32[]{:S(2)}) collective-permute-start(f32[128]{0:T(128)S(1)} %collective-permute-done.6), channel_id=1, source_target_pairs={{0,1},{1,2},{2,3},{3,4},{4,5},{5,6},{6,7},{7,8},{8,9},{9,10},{10,1... | collective-permute-start | bytes 1544 | tf_op jit(solution)/shard_map/ppermute | solution.py:53
  129.3 20.8 %collective-permute-start.8 = (f32[128]{0:T(128)S(1)}, f32[128]{0:T(128)S(1)}, u32[]{:S(2)}, u32[]{:S(2)}) collective-permute-start(f32[128]{0:T(128)S(1)} %collective-permute-done.7), channel_id=1, source_target_pairs={{0,1},{1,2},{2,3},{3,4},{4,5},{5,6},{6,7},{7,8},{8,9},{9,10},{10,1... | collective-permute-start | bytes 1544 | tf_op jit(solution)/shard_map/ppermute | solution.py:53
  150.1 5.7 %collective-permute-start.9 = (f32[128]{0:T(128)S(1)}, f32[128]{0:T(128)S(1)}, u32[]{:S(2)}, u32[]{:S(2)}) collective-permute-start(f32[128]{0:T(128)S(1)} %collective-permute-done.8), channel_id=1, source_target_pairs={{0,1},{1,2},{2,3},{3,4},{4,5},{5,6},{6,7},{7,8},{8,9},{9,10},{10,1... | collective-permute-start | bytes 1544 | tf_op jit(solution)/shard_map/ppermute | solution.py:53
  155.8 5.7 %collective-permute-start.10 = (f32[128]{0:T(128)S(1)}, f32[128]{0:T(128)S(1)}, u32[]{:S(2)}, u32[]{:S(2)}) collective-permute-start(f32[128]{0:T(128)S(1)} %collective-permute-done.9), channel_id=1, source_target_pairs={{0,1},{1,2},{2,3},{3,4},{4,5},{5,6},{6,7},{7,8},{8,9},{9,10},{10,1... | collective-permute-start | bytes 1544 | tf_op jit(solution)/shard_map/ppermute | solution.py:53
  161.5 5.7 %collective-permute-start.11 = (f32[128]{0:T(128)S(1)}, f32[128]{0:T(128)S(1)}, u32[]{:S(2)}, u32[]{:S(2)}) collective-permute-start(f32[128]{0:T(128)S(1)} %collective-permute-done.10), channel_id=1, source_target_pairs={{0,1},{1,2},{2,3},{3,4},{4,5},{5,6},{6,7},{7,8},{8,9},{9,10},{10,1... | collective-permute-start | bytes 1544 | tf_op jit(solution)/shard_map/ppermute | solution.py:53
  167.2 5.7 %collective-permute-start.12 = (f32[128]{0:T(128)S(1)}, f32[128]{0:T(128)S(1)}, u32[]{:S(2)}, u32[]{:S(2)}) collective-permute-start(f32[128]{0:T(128)S(1)} %collective-permute-done.11), channel_id=1, source_target_pairs={{0,1},{1,2},{2,3},{3,4},{4,5},{5,6},{6,7},{7,8},{8,9},{9,10},{10,1... | collective-permute-start | bytes 1544 | tf_op jit(solution)/shard_map/ppermute | solution.py:53
  172.9 5.7 %collective-permute-start.13 = (f32[128]{0:T(128)S(1)}, f32[128]{0:T(128)S(1)}, u32[]{:S(2)}, u32[]{:S(2)}) collective-permute-start(f32[128]{0:T(128)S(1)} %collective-permute-done.12), channel_id=1, source_target_pairs={{0,1},{1,2},{2,3},{3,4},{4,5},{5,6},{6,7},{7,8},{8,9},{9,10},{10,1... | collective-permute-start | bytes 1544 | tf_op jit(solution)/shard_map/ppermute | solution.py:53
  178.6 5.7 %collective-permute-start.14 = (f32[128]{0:T(128)S(1)}, f32[128]{0:T(128)S(1)}, u32[]{:S(2)}, u32[]{:S(2)}) collective-permute-start(f32[128]{0:T(128)S(1)} %collective-permute-done.13), channel_id=1, source_target_pairs={{0,1},{1,2},{2,3},{3,4},{4,5},{5,6},{6,7},{7,8},{8,9},{9,10},{10,1... | collective-permute-start | bytes 1544 | tf_op jit(solution)/shard_map/ppermute | solution.py:53
  185.2 1.0 copy-start.1
  225.2 2.9 %copy-start = (bf16[2048,128]{1,0:T(8,128)(2,1)S(1)}, bf16[2048,128]{1,0:T(8,128)(2,1)}, u32[]{:S(2)}) copy-start(bf16[2048,128]{1,0:T(8,128)(2,1)} %all_gather.33) | copy-start | bytes 1572868
